TPU v7x, 256 devices: a whole 4x4x8 slice. The times are simulated.
256 devices in a mesh: file: 8 (over x, core), blk: 32 (over z, y).
Axes of the slice: x: 4, y: 4, z: 8, core: 2. Of those that a mesh axis runs over, the one named last changes fastest.
Arguments:
- ctx_keys: bfloat16 [32768, 256], P(('file', 'blk')), parts along dimension 0, may hold values from -4 to 4
- ctx_values: bfloat16 [32768, 256], P(('file', 'blk')), parts along dimension 0, may hold values from -6 to 6
- middle_queries: bfloat16 [32768, 1792], P(('file', 'blk')), parts along dimension 0, may hold values from -40 to 40
- span_keys: bfloat16 [32768, 256], P(('file', 'blk')), parts along dimension 0, may hold values from -6 to 6
- span_values: bfloat16 [32768, 256], P(('file', 'blk')), parts along dimension 0, may hold values from -6 to 6
- span_len: int32 [256], P(('file', 'blk')), parts along dimension 0, may hold values from 36 to 128, as said below
- commit_pos: int32 [256, 2, 16], P(('file', 'blk')), parts along dimension 0, may hold values from 4 to 127, as said below
- commit_emb: bfloat16 [256, 2, 16, 3584], P(('file', 'blk')), parts along dimension 0, may hold values from -6 to 6
- w_key: bfloat16 [3584, 256], replicated, may hold values from -0.09375 to 0.09375
- w_value: bfloat16 [3584, 256], replicated, may hold values from -0.09375 to 0.09375
Outputs:
- span_out: bfloat16 [2, 32768, 1792], P(None, ('file', 'blk')), parts along dimension 1
There are 8 independent parts, one for each index of `file`. A program takes and returns all parts, laid end to end along the dimension named above; an argument that names none is the same for every part. Nothing has to cross between parts.
Inputs may be any that keep to these rules, and one draw needn't show every extreme that they name: `span_len`: some device's span fills all 128 slots in every draw. `commit_pos`: each device commits exactly 16 slots a step; a device's committed slots are distinct over all steps and lie below that device's span length.
All inputs are finite; a program needn't handle non-finite values.
Results may differ from a plain program's by a relative error of at most 0.0067.
Values may be sent and summed in bfloat16 or wider, within the bound.
No kernel may reach another device: no remote copies, remote signals or barrier semaphores. Data moves between devices by JAX's collectives and lax.ppermute only.
A program may use at most 256 MiB of HBM per device.

v0:
```python
import math

import jax
import jax.numpy as jnp
from jax import lax
from jax.sharding import PartitionSpec as P

HEAD_WIDTH = 128
KEY_VALUE_HEADS = 2
STEPS = 2
QUERY_PER_KEY = 7


def attend_piece(carried, heads_of_queries, key_matrix, value_matrix, live_keys):
    row_max, row_sum, weighted = carried
    row_count = key_matrix.shape[0]
    heads_of_keys = key_matrix.reshape(row_count, KEY_VALUE_HEADS, HEAD_WIDTH)
    heads_of_values = value_matrix.reshape(row_count, KEY_VALUE_HEADS, HEAD_WIDTH)
    scores = jnp.einsum(
        "sgrd,kgd->gsrk", heads_of_queries, heads_of_keys, preferred_element_type=jnp.float32
    ) / math.sqrt(HEAD_WIDTH)
    scores = jnp.where(live_keys[None, None, None, :], scores, -jnp.inf)
    new_max = jnp.maximum(row_max, jnp.max(scores, axis=-1))
    expw = jnp.exp(scores - new_max[..., None])
    row_sum = jnp.sum(expw, axis=-1)
    weighted = jnp.einsum(
        "gsrk,kgd->gsrd",
        expw.astype(jnp.bfloat16),
        heads_of_values,
        preferred_element_type=jnp.float32,
    )
    return (new_max, row_sum, weighted)


def per_device(
    ctx_keys,
    ctx_values,
    middle_queries,
    span_keys,
    span_values,
    span_len,
    commit_pos,
    commit_emb,
    w_key,
    w_value,
):
    local_rows = middle_queries.shape[0]
    slots = jnp.arange(local_rows, dtype=jnp.int32)
    live_here = slots < span_len[0]
    span_flags = live_here.astype(jnp.bfloat16)
    heads_of_queries = middle_queries.reshape(
        local_rows, KEY_VALUE_HEADS, QUERY_PER_KEY, HEAD_WIDTH
    )
    starting = (
        jnp.full((KEY_VALUE_HEADS, local_rows, QUERY_PER_KEY), -1e30, jnp.float32),
        jnp.zeros((KEY_VALUE_HEADS, local_rows, QUERY_PER_KEY), jnp.float32),
        jnp.zeros((KEY_VALUE_HEADS, local_rows, QUERY_PER_KEY, HEAD_WIDTH), jnp.float32),
    )
    keys_now = span_keys
    values_now = span_values
    committed = jnp.zeros((local_rows,), bool)
    attention_outputs = []
    for number in range(STEPS):
        embedded = commit_emb[0, number]
        new_keys = jnp.dot(embedded, w_key, preferred_element_type=jnp.float32).astype(jnp.bfloat16)
        new_values = jnp.dot(embedded, w_value, preferred_element_type=jnp.float32).astype(
            jnp.bfloat16
        )
        slot_ids = commit_pos[0, number]
        committed = committed | jnp.any(slots[:, None] == slot_ids[None, :], axis=1)
        active = live_here & ~committed
        keys_now = keys_now.at[slot_ids].set(new_keys)
        values_now = values_now.at[slot_ids].set(new_values)
        joined_keys = jnp.concatenate([ctx_keys, keys_now])
        joined_values = jnp.concatenate([ctx_values, values_now])
        joined_flags = jnp.concatenate([jnp.ones((ctx_keys.shape[0],), jnp.bfloat16), span_flags])
        row_max, row_sum, weighted = attend_piece(
            starting,
            heads_of_queries,
            lax.all_gather(joined_keys, "blk", axis=0, tiled=True),
            lax.all_gather(joined_values, "blk", axis=0, tiled=True),
            lax.all_gather(joined_flags, "blk", axis=0, tiled=True) > 0.5,
        )
        attention_output = (
            (weighted / row_sum[..., None])
            .transpose(1, 0, 2, 3)
            .reshape(local_rows, KEY_VALUE_HEADS * QUERY_PER_KEY * HEAD_WIDTH)
        )
        attention_outputs.append(
            jnp.where(active[:, None], attention_output, 0.0).astype(jnp.bfloat16)
        )
    return jnp.stack(attention_outputs)


def solution(mesh):
    in_specs = (
        P(("file", "blk"), None),
        P(("file", "blk"), None),
        P(("file", "blk"), None),
        P(("file", "blk"), None),
        P(("file", "blk"), None),
        P(("file", "blk")),
        P(("file", "blk"), None, None),
        P(("file", "blk"), None, None, None),
        P(),
        P(),
    )
    out_specs = P(None, ("file", "blk"), None)
    return jax.shard_map(
        per_device, mesh=mesh, in_specs=in_specs, out_specs=out_specs, check_vma=False
    )
```

profile of v0, /device:TPU:4, one launch (start us, length us, event | category | flops | bytes accessed | tf_op | source)
XLA Modules:
  0.0 381.7 jit_solution(502001056477325090)
XLA Ops:
  6.5 0.0 copy-start
  6.5 0.0 all-gather.6.cloned.1.call-start
  6.5 1.0 copy.77
  7.5 0.8 copy.78
  8.4 0.0 copy-done
  8.4 1.2 convolution_convert_fusion.3
  9.6 1.3 convolution_convert_fusion.1
  10.9 0.8 fusion.35
  11.6 0.7 scatter_fusion
  12.4 0.7 scatter_fusion.2
  13.1 1.5 pad_maximum_fusion.4
  14.6 0.0 all-gather.6.cloned.1.call-update
  14.7 0.0 all-gather.10.cloned.1.call-start
  14.7 0.7 all-gather.10.cloned.1.call-update
  15.4 0.0 all-gather.8.cloned.1.call-start
  15.5 1.9 convolution_convert_fusion.2
  17.4 0.7 scatter_fusion.1
  18.1 1.9 convolution_convert_fusion
  20.1 0.7 scatter_fusion.3
  20.8 1.5 pad_maximum_fusion.2
  22.3 0.0 all-gather.8.cloned.1.call-update
  22.4 0.0 all-gather.12.cloned.1.call-start
  22.4 0.5 all-gather.12.cloned.1.call-update
  22.9 0.8 slice_bitcast_fusion
  23.7 0.1 fusion.32
  23.8 0.1 fusion.33
  24.5 0.5 not_and_fusion.1
  25.1 46.3 %all-gather = bf16[32,1,256]{2,1,0:T(2,128)(2,1)S(1)} all-gather(bf16[1,1,256]{2,1,0:T(2,128)(2,1)S(1)} %reshape.208), channel_id=1, replica_groups=mesh['file'=8,'blk'=32] {'blk'}, dimensions={0}, use_global_device_ids=true | all-gather | bytes 16896 | tf_op jit(solution)/shard_map/all_gather | solution.py:82
  71.3 0.1 compare_reduce_fusion
  71.5 1.3 copy.46
  72.8 26.8 %all-gather.6.cloned.1.call-done = bf16[8192,256]{1,0:T(8,128)(2,1)} async-done(((bf16[256,256]{1,0:T(8,128)(2,1)}), bf16[8192,256]{1,0:T(8,128)(2,1)}) %all-gather.6.cloned.1.call-update) | async-done | bytes 4194320 | tf_op jit(solution)/shard_map/all_gather | solution.py:80
  99.6 6.4 %copy.45 = bf16[8192,256]{0,1:T(8,128)(2,1)} copy(bf16[8192,256]{1,0:T(8,128)(2,1)} %all-gather.6.cloned.1.call-done) | data formatting | bytes 8388608 | tf_op jit(solution)/shard_map/all_gather | solution.py:80
  106.0 24.6 %bitcast_reduce_fusion.1 = (f32[2,128,7]{1,2,0:T(8,128)S(1)}, f32[2,8192,128,7]{2,1,3,0:T(8,128)}) fusion(pred[8192]{0:T(1024)(128)(4,1)S(1)} %reshape.211, bf16[8192,2,128,1]{0,2,3,1:T(8,128)(2,1)} %bitcast.95, bf16[128,2,7,128]{0,3,2,1:T(8,128)(2,1)S(1)} %bitcast.99), kind=kOutput, calls=%fused_computation.8 | convolution fusion | flops 3802134784 | bytes 63388672 | tf_op jit(solution)/shard_map/sgrd,kgd->gsrk/dot_general | solution.py:19
  130.5 50.8 %all-gather.10.cloned.1.call-done = bf16[8192,256]{1,0:T(8,128)(2,1)} async-done(((bf16[256,256]{1,0:T(8,128)(2,1)}), bf16[8192,256]{1,0:T(8,128)(2,1)}) %all-gather.10.cloned.1.call-update) | async-done | bytes 4194320 | tf_op jit(solution)/shard_map/all_gather | solution.py:80
  181.3 6.4 %copy.52 = bf16[8192,256]{0,1:T(8,128)(2,1)} copy(bf16[8192,256]{1,0:T(8,128)(2,1)} %all-gather.10.cloned.1.call-done) | data formatting | bytes 8388608 | tf_op jit(solution)/shard_map/all_gather | solution.py:80
  187.7 49.4 %fusion.2 = (f32[2,128,7]{1,2,0:T(8,128)S(1)}, f32[2,128,7]{1,2,0:T(8,128)S(1)}, f32[2,8192,128,7]{2,1,3,0:T(8,128)}) fusion(f32[2,8192,128,7]{2,1,3,0:T(8,128)} %get-tuple-element.18, f32[2,128,7]{1,2,0:T(8,128)S(1)} %broadcast_maximum_fusion.1, pred[8192]{0:T(1024)(128)(4,1)S(1)} %reshape.211, bf16[8192,2,128,1]{0,2,3,1:T(8,128)(2,1)} %bitcast.96, ...), kind=kOutput, calls=%fused_computation.12 | convolution fusion | flops 3860853248 | bytes 122123264 | tf_op jit(solution)/shard_map/sgrd,kgd->gsrk/dot_general | solution.py:19
  237.0 26.0 %all-gather.8.cloned.1.call-done = bf16[8192,256]{1,0:T(8,128)(2,1)} async-done(((bf16[256,256]{1,0:T(8,128)(2,1)}), bf16[8192,256]{1,0:T(8,128)(2,1)}) %all-gather.8.cloned.1.call-update) | async-done | bytes 4194320 | tf_op jit(solution)/shard_map/all_gather | solution.py:81
  263.0 6.4 %copy.49 = bf16[8192,256]{0,1:T(8,128)(2,1)} copy(bf16[8192,256]{1,0:T(8,128)(2,1)} %all-gather.8.cloned.1.call-done) | data formatting | bytes 8388608 | tf_op jit(solution)/shard_map/all_gather | solution.py:81
  269.4 22.8 %fusion.21 = bf16[128,2,7,128]{0,3,2,1:T(8,128)(2,1)S(1)} fusion(bf16[8192,2,128,1]{0,2,3,1:T(8,128)(2,1)} %bitcast.98, f32[2,8192,128,7]{2,1,3,0:T(8,128)} %get-tuple-element.18, f32[2,128,7]{1,2,0:T(8,128)S(1)} %broadcast_maximum_fusion.1, pred[8192]{0:T(1024)(128)(4,1)S(1)} %reshape.211, f32[128,2,7]{0,2,1:T(8,128)S(1)} %bitcast.104), kind=kOutput, calls=%fused_computation.23 | convolution fusion | flops 3817275392 | bytes 63395840 | tf_op jit(solution)/shard_map/gsrk,kgd->gsrd/dot_general | solution.py:26
  292.2 0.2 copy.51
  292.4 0.0 copy-start.1
  292.5 19.4 %fusion.4 = f32[2,128,7]{1,2,0:T(8,128)S(1)} fusion(f32[2,8192,128,7]{2,1,3,0:T(8,128)} %get-tuple-element.19, f32[2,128,7]{1,2,0:T(8,128)S(1)} %broadcast_maximum_fusion, pred[8192]{0:T(1024)(128)(4,1)S(1)} %reshape.211), kind=kLoop, calls=%fused_computation.14 | loop fusion | flops 58718464 | bytes 58742784 | tf_op jit(solution)/shard_map/reduce_sum | solution.py:25
  311.9 0.0 copy-start.3
  311.9 0.0 copy-start.2
  311.9 32.7 %all-gather.12.cloned.1.call-done = bf16[8192,256]{1,0:T(8,128)(2,1)} async-done(((bf16[256,256]{1,0:T(8,128)(2,1)}), bf16[8192,256]{1,0:T(8,128)(2,1)}) %all-gather.12.cloned.1.call-update) | async-done | bytes 4194320 | tf_op jit(solution)/shard_map/all_gather | solution.py:81
  344.6 6.4 %copy.55 = bf16[8192,256]{0,1:T(8,128)(2,1)} copy(bf16[8192,256]{1,0:T(8,128)(2,1)} %all-gather.12.cloned.1.call-done) | data formatting | bytes 8388608 | tf_op jit(solution)/shard_map/all_gather | solution.py:81
  351.0 22.7 %fusion.18 = bf16[128,2,7,128]{0,3,2,1:T(8,128)(2,1)S(1)} fusion(bf16[8192,2,128,1]{0,2,3,1:T(8,128)(2,1)} %bitcast.97, f32[2,8192,128,7]{2,1,3,0:T(8,128)} %get-tuple-element.19, f32[2,128,7]{1,2,0:T(8,128)S(1)} %broadcast_maximum_fusion, pred[8192]{0:T(1024)(128)(4,1)S(1)} %reshape.211, f32[128,2,7]{0,2,1:T(8,128)S(1)} %bitcast.103), kind=kOutput, calls=%fused_computation.22 | convolution fusion | flops 3817275392 | bytes 63395840 | tf_op jit(solution)/shard_map/gsrk,kgd->gsrd/dot_general | solution.py:26
  373.7 0.2 copy.57
  373.9 0.0 copy-done.3
  373.9 0.1 select_convert_fusion.1
  374.0 0.0 copy-done.2
  374.1 0.1 select_convert_fusion
  374.2 1.0 pad_maximum_fusion
  375.2 0.0 copy-done.1
  (7 shorter events, 0.1 us)
Async XLA Ops:
  6.5 1.8 copy-start
  6.5 93.1 %all-gather.6.cloned.1.call-start = ((), (), s32[]{:S(2)}) async-start(), calls=%async_computation | async-start | bytes 4325376 | tf_op jit(solution)/shard_map/all_gather | solution.py:80
  14.7 166.6 %all-gather.10.cloned.1.call-start = ((), (), s32[]{:S(2)}) async-start(), calls=%async_computation.2 | async-start | bytes 4325376 | tf_op jit(solution)/shard_map/all_gather | solution.py:80
  15.4 247.6 %all-gather.8.cloned.1.call-start = ((), (), s32[]{:S(2)}) async-start(), calls=%async_computation.1 | async-start | bytes 4325376 | tf_op jit(solution)/shard_map/all_gather | solution.py:81
  22.4 322.2 %all-gather.12.cloned.1.call-start = ((), (), s32[]{:S(2)}) async-start(), calls=%async_computation.3 | async-start | bytes 4325376 | tf_op jit(solution)/shard_map/all_gather | solution.py:81
  292.4 82.8 %copy-start.1 = (bf16[3584,256]{1,0:T(8,128)(2,1)S(1)}, bf16[3584,256]{1,0:T(8,128)(2,1)}, u32[]{:S(2)}) copy-start(bf16[3584,256]{1,0:T(8,128)(2,1)} %param.18) | copy-start | bytes 5505028
  311.9 62.0 %copy-start.3 = (pred[128]{0:T(512)(128)(4,1)S(1)}, pred[128]{0:T(512)(128)(4,1)}, u32[]{:S(2)}) copy-start(pred[128]{0:T(512)(128)(4,1)} %get-tuple-element.15) | copy-start | bytes 388
  311.9 62.2 %copy-start.2 = (pred[128]{0:T(512)(128)(4,1)S(1)}, pred[128]{0:T(512)(128)(4,1)}, u32[]{:S(2)}) copy-start(pred[128]{0:T(512)(128)(4,1)} %get-tuple-element.16) | copy-start | bytes 388
Sparse Core Ops, SparseCore 0:
  14.8 84.7 all-gather.5
  102.2 79.0 all-gather.9
  183.9 79.0 all-gather.7
  265.5 79.0 all-gather.11
where the time goes:
time: 383 us; the launch traced here: 382 us
  waiting for transfers between devices  138 us (36%)
  matrix products  126 us (33%)
  blocking collectives  46.3 us (12%)
  local copies, waits for them, and re-layouts  32.7 us (9%)
  other arithmetic  25.4 us (7%)
  between operations  13.9 us (4%)
    all_gather x2, waiting for transfers between devices, per_device(): lax.all_gather(joined_keys, 'blk', axis=0, tiled=True)  77.6 us
    dot_general x2, matrix products, attend_piece(): jnp.einsum('sgrd,kgd->gsrk', heads_of_queries, heads_of_keys, preferred_e...  73.9 us
    all_gather x2, waiting for transfers between devices, per_device(): lax.all_gather(joined_values, 'blk', axis=0, tiled=True)  58.7 us
    all_gather x1, blocking collectives, per_device(): lax.all_gather(joined_flags, 'blk', axis=0, tiled=True) > 0.5  46.3 us
    dot_general x2, matrix products, attend_piece(): jnp.einsum('gsrk,kgd->gsrd', expw.astype(jnp.bfloat16), heads_of_values,...  45.5 us
    reduce_sum x1, other arithmetic, attend_piece(): row_sum = jnp.sum(expw, axis=-1)  19.4 us
    all_gather x2, local copies, waits for them, and re-layouts, per_device(): lax.all_gather(joined_keys, 'blk', axis=0, tiled=True)  12.7 us
    all_gather x2, local copies, waits for them, and re-layouts, per_device(): lax.all_gather(joined_values, 'blk', axis=0, tiled=True)  12.7 us
  transfers between devices with their start and end apart: 4, of which 4 were waited for; matrix products, arithmetic and copies ran while one was open for 38% of the time, Pallas kernels for 0%

commit v1 on v0

v1 whole, which is shorter than its diff:
```python
import functools
import math

import jax
import jax.numpy as jnp
from jax import lax
from jax.experimental import pallas as pl
from jax.experimental.pallas import tpu as pltpu
from jax.sharding import PartitionSpec as P

BF16 = jnp.bfloat16
F32 = jnp.float32
HEAD = 128
GROUPS = 2
PER_GROUP = 7
HEADS = GROUPS * PER_GROUP
COMMIT = 16
SLOTS = 128
COMMON = SLOTS - COMMIT
BOTH = SLOTS - 2 * COMMIT
KVW = GROUPS * HEAD
PAIR = 2 * KVW
ROWS = PER_GROUP * COMMON
MARK = 1e30
SCALE = math.log2(math.e) / math.sqrt(HEAD)
VMEM = pl.BlockSpec(memory_space=pltpu.VMEM)
SMEM = pl.BlockSpec(memory_space=pltpu.SMEM)


def vmem_params(mib):
    return pltpu.CompilerParams(vmem_limit_bytes=mib << 20)


def named_slots(pos_ref, step):
    slot = lax.broadcasted_iota(jnp.int32, (SLOTS, COMMIT), 0)
    return (slot == pos_ref[0, step : step + 1, :]).astype(F32)


def rank_of(flag):
    row = lax.broadcasted_iota(jnp.int32, (SLOTS, SLOTS), 0)
    col = lax.broadcasted_iota(jnp.int32, (SLOTS, SLOTS), 1)
    return jnp.dot((col < row).astype(BF16), flag.astype(BF16), preferred_element_type=F32)


def lanes():
    return lax.broadcasted_iota(jnp.int32, (SLOTS, SLOTS), 1).astype(F32)


def flag_of(named):
    return jnp.broadcast_to(jnp.max(named, axis=1, keepdims=True), (SLOTS, SLOTS))


def select_rows(chosen, rows):
    return lax.dot_general(
        chosen.astype(BF16), rows, (((0,), (0,)), ((), ())), preferred_element_type=F32
    ).astype(BF16)


def span_rows(len_ref, pos_ref, emb_ref, wk_ref, wv_ref, sk_ref, sv_ref, out_ref, base):
    named0 = named_slots(pos_ref, 0)
    named1 = named_slots(pos_ref, 1)
    in0 = flag_of(named0)
    stay = 1.0 - flag_of(named1)
    chosen = jnp.where(rank_of(stay) == lanes(), stay, 0.0)
    dead = lax.broadcasted_iota(jnp.int32, (SLOTS, KVW), 0) >= len_ref[0]
    emb = emb_ref[0].reshape(2 * COMMIT, emb_ref.shape[3])
    for part, (w_ref, s_ref) in enumerate(((wk_ref, sk_ref), (wv_ref, sv_ref))):
        new = jnp.dot(emb, w_ref[...], preferred_element_type=F32).astype(BF16)
        put = jnp.dot(named0.astype(BF16), new[:COMMIT], preferred_element_type=F32)
        now = jnp.where(
            jnp.concatenate([in0, in0], axis=1) > 0.5, put, s_ref[...].astype(F32)
        )
        filler = now[0:1, :] if part == 0 else jnp.full((1, KVW), MARK, F32)
        now = jnp.where(dead, filler, now).astype(BF16)
        cols = slice(part * KVW, (part + 1) * KVW)
        out_ref[base : base + COMMON, cols] = select_rows(chosen, now)[:COMMON]
        out_ref[base + COMMON : base + SLOTS, cols] = select_rows(named1, now)
        out_ref[base + SLOTS : base + SLOTS + COMMIT, cols] = new[COMMIT:]


def prepare_kernel(
    len_ref, pos_ref, emb_ref, wk_ref, wv_ref, ck_ref, cv_ref, sk_ref, sv_ref, out_ref
):
    out_ref[0:SLOTS, 0:KVW] = ck_ref[...]
    out_ref[0:SLOTS, KVW:PAIR] = cv_ref[...]
    span_rows(len_ref, pos_ref, emb_ref, wk_ref, wv_ref, sk_ref, sv_ref, out_ref, SLOTS)


def query_order(pos_ref):
    in0 = flag_of(named_slots(pos_ref, 0))
    in1 = flag_of(named_slots(pos_ref, 1))
    never = (1.0 - in0) * (1.0 - in1)
    first = jnp.where(rank_of(never) == lanes(), never, 0.0)
    second = jnp.where(rank_of(in1) + float(BOTH) == lanes(), in1, 0.0)
    return first, second


def queries_kernel(pos_ref, mq_ref, out_ref):
    first, second = query_order(pos_ref)
    picked = select_rows(first + second, mq_ref[...])
    for head in range(HEADS):
        out_ref[head * COMMON : (head + 1) * COMMON, :] = picked[
            :COMMON, head * HEAD : (head + 1) * HEAD
        ]


def attend(q, keys, values, old_acc, old_max):
    marked = values > MARK / 2
    zero = jnp.zeros_like(values)
    values = jnp.concatenate(
        [jnp.where(marked, zero, values), jnp.where(marked, zero, jnp.ones_like(values))], axis=1
    )
    scores = lax.dot_general(q, keys, (((1,), (1,)), ((), ())), preferred_element_type=F32)
    new_max = jnp.maximum(old_max, jnp.max(scores, axis=1, keepdims=True))
    weights = jnp.exp2((scores - new_max[:, :1]) * SCALE).astype(BF16)
    keep = jnp.exp2((old_max - new_max) * SCALE)
    gained = jnp.dot(weights, values, preferred_element_type=F32)
    return old_acc * jnp.concatenate([keep, keep], axis=1) + gained, new_max


def head_cols(group, part):
    return slice(part * KVW + group * HEAD, part * KVW + (group + 1) * HEAD)


def attention_kernel(
    blocks, len_ref, pos_ref, q_ref, kv_ref, out_ref, acc, top, shared, old, new, rows_out
):
    step = pl.program_id(0)
    size = SLOTS + COMMON

    @pl.when(step == 0)
    def _():
        acc[...] = jnp.zeros_like(acc)
        top[...] = jnp.full_like(top, -1e30)

    for b in range(blocks):
        at = b * (2 * SLOTS + COMMIT)
        shared[b * size : (b + 1) * size, :] = kv_ref[at : at + size, :]
        where = pl.ds(pl.multiple_of((step * blocks + b) * COMMIT, COMMIT), COMMIT)
        old[where, :] = kv_ref[at + size : at + 2 * SLOTS, :]
        new[where, :] = kv_ref[at + 2 * SLOTS : at + 2 * SLOTS + COMMIT, :]

    for group in range(GROUPS):
        for head in range(PER_GROUP):
            at = (group * PER_GROUP + head) * COMMON
            rows = slice(at, at + COMMON)
            acc[rows, :], top[rows, :] = attend(
                q_ref[rows, :],
                shared[:, head_cols(group, 0)],
                shared[:, head_cols(group, 1)],
                acc[rows, :],
                top[rows, :],
            )

    @pl.when(step == pl.num_programs(0) - 1)
    def _():
        first, second = query_order(pos_ref)
        live = lax.broadcasted_iota(jnp.int32, (SLOTS, SLOTS), 0) < len_ref[0]
        rows_out[COMMON:, :] = jnp.zeros((COMMIT, HEADS * HEAD), BF16)
        for number, extra in enumerate((old, new)):
            for group in range(GROUPS):
                for head in range(PER_GROUP):
                    index = group * PER_GROUP + head
                    rows = slice(index * COMMON, (index + 1) * COMMON)
                    full, _ = attend(
                        q_ref[rows, :],
                        extra[:, head_cols(group, 0)],
                        extra[:, head_cols(group, 1)],
                        acc[rows, :],
                        top[rows, :],
                    )
                    rows_out[:COMMON, index * HEAD : (index + 1) * HEAD] = (
                        full[:, :HEAD] / full[:, HEAD:]
                    ).astype(BF16)
            place = jnp.where(live, first + second if number == 0 else first, 0.0).astype(BF16)
            out_ref[number] = jnp.dot(
                place, rows_out[...], preferred_element_type=F32
            ).astype(BF16)


def per_device(
    ctx_keys,
    ctx_values,
    middle_queries,
    span_keys,
    span_values,
    span_len,
    commit_pos,
    commit_emb,
    w_key,
    w_value,
):
    payload = pl.pallas_call(
        prepare_kernel,
        out_shape=jax.ShapeDtypeStruct((2 * SLOTS + COMMIT, PAIR), BF16),
        in_specs=[SMEM] + [VMEM] * 8,
        out_specs=VMEM,
        compiler_params=vmem_params(24),
        name="prepare",
    )(
        span_len,
        commit_pos,
        commit_emb,
        w_key,
        w_value,
        ctx_keys,
        ctx_values,
        span_keys,
        span_values,
    )
    gathered = lax.all_gather(payload, "blk", axis=0, tiled=True)
    queries = pl.pallas_call(
        queries_kernel,
        out_shape=jax.ShapeDtypeStruct((HEADS * COMMON, HEAD), BF16),
        in_specs=[VMEM, VMEM],
        out_specs=VMEM,
        compiler_params=vmem_params(24),
        name="queries",
    )(commit_pos, middle_queries)
    count = gathered.shape[0] // payload.shape[0]
    blocks = 8
    whole = lambda shape: pl.BlockSpec(shape, lambda i: (0,) * len(shape))
    return pl.pallas_call(
        functools.partial(attention_kernel, blocks),
        out_shape=jax.ShapeDtypeStruct((2, SLOTS, HEADS * HEAD), BF16),
        grid=(count // blocks,),
        in_specs=[
            SMEM,
            whole(commit_pos.shape),
            whole(queries.shape),
            pl.BlockSpec((blocks * payload.shape[0], PAIR), lambda i: (i, 0)),
        ],
        out_specs=whole((2, SLOTS, HEADS * HEAD)),
        scratch_shapes=[
            pltpu.VMEM((HEADS * COMMON, 2 * HEAD), F32),
            pltpu.VMEM((HEADS * COMMON, HEAD), F32),
            pltpu.VMEM((blocks * (SLOTS + COMMON), PAIR), BF16),
            pltpu.VMEM((count * COMMIT, PAIR), BF16),
            pltpu.VMEM((count * COMMIT, PAIR), BF16),
            pltpu.VMEM((SLOTS, HEADS * HEAD), BF16),
        ],
        compiler_params=vmem_params(50),
        name="attention",
    )(span_len, commit_pos, queries, gathered)


def solution(mesh):
    both = ("file", "blk")
    in_specs = (
        P(both, None),
        P(both, None),
        P(both, None),
        P(both, None),
        P(both, None),
        P(both),
        P(both, None, None),
        P(both, None, None, None),
        P(),
        P(),
    )
    return jax.shard_map(
        per_device, mesh=mesh, in_specs=in_specs, out_specs=P(None, both, None), check_vma=False
    )
```

time: 383 us -> 167 us (0.44)
  matrix products: 126 us -> 0 us
  blocking collectives: 46.3 us -> 0 us
  Pallas kernels: 0 us -> 40.1 us
  waiting for transfers between devices: 138 us -> 104 us
  other arithmetic: 25.4 us -> 0 us
  local copies, waits for them, and re-layouts: 32.7 us -> 7.97 us
    dot_general x8 -> x0, matrix products: 126 us -> none  [the longest x2 73.9 us: attend_piece(): jnp.einsum('sgrd,kgd->gsrk', heads_of_queries, heads_of_keys, preferred_e...]
    all_gather x1 -> x0, blocking collectives: 46.3 us -> none  [per_device(): lax.all_gather(joined_flags, 'blk', axis=0, tiled=True) > 0.5]
    pallas_call x0 -> x3, Pallas kernels: none -> 40.1 us  [the longest x1 37.2 us: per_device(): pl.pallas_call(functools.partial(attention_kernel, blocks), out_shape=jax...]
    all_gather x4 -> x1, waiting for transfers between devices: 136 us -> 104 us  [per_device(): gathered = lax.all_gather(payload, 'blk', axis=0, tiled=True)]
    all_gather x4 -> x0, local copies, waits for them, and re-layouts: 25.5 us -> none  [the longest x2 12.7 us: per_device(): lax.all_gather(joined_keys, 'blk', axis=0, tiled=True)]
    reduce_sum x1 -> x0, other arithmetic: 19.4 us -> none  [attend_piece(): row_sum = jnp.sum(expw, axis=-1)]
    unnamed x14 -> x20, local copies, waits for them, and re-layouts: 3.13 us -> 7.97 us
  transfers between devices with their start and end apart: 4 -> 1, of which waited for: 4 -> 1; matrix products, arithmetic and copies ran while one was open for 38% -> 0% of each run, Pallas kernels for 0% -> 0%
where the time goes in v1:
time: 167 us; the launch traced here: 166 us
  waiting for transfers between devices  104 us (62%)
  Pallas kernels  40.1 us (24%)
  between operations  14.1 us (8%)
  local copies, waits for them, and re-layouts  7.97 us (5%)
    all_gather x1, waiting for transfers between devices, per_device(): gathered = lax.all_gather(payload, 'blk', axis=0, tiled=True)  104 us
    pallas_call x1, Pallas kernels, per_device(): pl.pallas_call(functools.partial(attention_kernel, blocks), out_shape=jax...  37.2 us
    unnamed x20, local copies, waits for them, and re-layouts  7.97 us
  transfers between devices with their start and end apart: 1, of which 1 were waited for; matrix products, arithmetic and copies ran while one was open for 0% of the time, Pallas kernels for 0%

profile of v1, /device:TPU:4, one launch (start us, length us, event | category | flops | bytes accessed | tf_op | source)
XLA Modules:
  0.0 165.8 jit_solution(12517403422764074007)
XLA Ops:
  6.5 0.0 all-gather.2.cloned.1.call-start
  7.2 0.0 copy-start
  7.2 1.5 copy-done
  8.7 0.0 copy-start.1
  8.7 1.5 copy-done.1
  10.2 0.0 copy-start.3
  10.2 0.9 copy-done.3
  11.1 0.0 copy-start.4
  11.1 0.8 copy-done.4
  12.0 0.0 copy-start.5
  12.0 0.8 copy-done.5
  12.8 0.0 copy-start.6
  12.8 0.8 copy-done.6
  13.6 0.0 copy-start.7
  13.7 0.8 copy-done.7
  14.5 0.0 copy-start.8
  14.5 0.7 copy-done.8
  15.2 0.0 copy-start.2
  15.2 0.0 copy-start.9
  15.2 2.4 %prepare.1 = bf16[272,512]{1,0:T(8,128)(2,1)} custom-call(s32[1]{0:T(128)S(6)} %copy.11.len_ref, s32[1,2,16]{2,1,0:T(2,128)S(1)} %copy-done.8, bf16[1,2,16,3584]{3,2,1,0:T(8,128)(2,1)S(1)} %copy-done.3, bf16[3584,256]{1,0:T(8,128)(2,1)S(1)} %copy-done, bf16[3584,256]{1,0:T(8,128)(2,1)S(1)} %copy-done.1, bf16[128,256]{1,0:T(8,128)(2,1)S(1)} %copy-done.4, ...), custom_call_target="tpu_custom_call" | custom-call | tf_op jit(solution)/shard_map/prepare/pallas_call | solution.py:193
  17.5 0.0 all-gather.2.cloned.1.call-update
  17.5 0.0 copy-done.2
  17.6 0.0 copy-done.9
  17.6 0.6 queries.1.q_ref
  18.1 103.7 %all-gather.2.cloned.1.call-done.kv_ref = bf16[8704,512]{1,0:T(8,128)(2,1)} async-done(((bf16[272,512]{1,0:T(8,128)(2,1)}), bf16[8704,512]{1,0:T(8,128)(2,1)}) %all-gather.2.cloned.1.call-update) | async-done | bytes 8912912 | tf_op jit(solution)/shard_map/all_gather | solution.py:211
  121.8 37.2 %attention.1 = bf16[2,128,1792]{2,1,0:T(8,128)(2,1)} custom-call(s32[1]{0:T(128)S(6)} %copy.11.len_ref, s32[1,2,16]{2,1,0:T(2,128)S(1)} %copy-done.9, bf16[1568,128]{1,0:T(8,128)(2,1)S(1)} %queries.1.q_ref, bf16[8704,512]{1,0:T(8,128)(2,1)} %all-gather.2.cloned.1.call-done.kv_ref), custom_call_target="tpu_custom_call" | custom-call | tf_op jit(solution)/shard_map/attention/pallas_call | solution.py:223
Async XLA Ops:
  6.5 115.3 %all-gather.2.cloned.1.call-start = ((), (), s32[]{:S(2)}) async-start(), calls=%async_computation | async-start | bytes 9191424 | tf_op jit(solution)/shard_map/all_gather | solution.py:211
  7.2 1.5 copy-start
  8.7 1.5 copy-start.1
  10.2 0.9 copy-start.3
  11.1 0.8 copy-start.4
  12.0 0.8 copy-start.5
  12.8 0.8 copy-start.6
  13.6 0.8 copy-start.7
  14.5 0.7 copy-start.8
  15.2 2.4 %copy-start.2 = (bf16[128,1792]{1,0:T(8,128)(2,1)S(1)}, bf16[128,1792]{1,0:T(8,128)(2,1)}, u32[]{:S(2)}) copy-start(bf16[128,1792]{1,0:T(8,128)(2,1)} %mq_ref.1) | copy-start | bytes 1376260
  15.2 2.4 %copy-start.9 = (s32[1,2,16]{2,1,0:T(2,128)S(1)}, s32[1,2,16]{2,1,0:T(2,128)}, u32[]{:S(2)}) copy-start(s32[1,2,16]{2,1,0:T(2,128)} %pos_ref.5) | copy-start | bytes 388
Sparse Core Ops, SparseCore 0:
  17.7 104.1 all-gather.1
